TPU v7x, 512 devices: a whole 4x4x16 slice. The times are simulated.
512 devices in a mesh: lat: 16 (over x, y_lo, core), lon: 32 (over y_hi, z).
Axes of the slice: x: 4, y: 4 (y_hi: 2, y_lo: 2; y = y_hi * 2 + y_lo), z: 16, core: 2. Of those that a mesh axis runs over, the one named last changes fastest.
Arguments:
- features: bfloat16 [64, 1024, 256], P('lat', 'lon'), may hold values from -6 to 6
- cotangent: bfloat16 [64, 1024, 256], P('lat', 'lon'), may hold values from -6 to 6
- weight: bfloat16 [4, 256, 256], replicated, may hold values from -0.1875 to 0.1875
- filter_taps: bfloat16 [64, 4, 5, 64], P('lat'), may hold values from -6 to 6
- lat_ext: int32 [64], P('lat'), may hold values from 1 to 3, as said below
- lon_count: int32 [64], P('lat'), may hold values from 1 to 32, as said below
Outputs:
- output: bfloat16 [64, 1024, 256], P('lat', 'lon')
- field_grad: bfloat16 [64, 1024, 256], P('lat', 'lon')
- weight_grad: float32 [4, 256, 256], replicated
Inputs may be any that keep to these rules, and one draw needn't show every extreme that they name: `lat_ext`: a row uses the latitude offsets whose magnitude is below its entry. `lon_count`: a row uses the longitude offsets whose magnitude is below its entry.
All inputs are finite; a program needn't handle non-finite values.
Results may differ from a plain program's by a relative error of at most 0.006.
Values may be sent and summed in bfloat16 or wider, within the bound.
A program may use at most 64 MiB of HBM per device.

v0:
```python
import math
import jax
import jax.numpy as jnp
from jax import lax
from jax.sharding import PartitionSpec as P


def extended(cells, sides, width, closed):
    for axis, dim in sides:
        count = lax.axis_size(axis)
        ends = count if closed else count - 1
        head = lax.slice_in_dim(cells, 0, width, axis=dim)
        tail = lax.slice_in_dim(cells, cells.shape[dim] - width, cells.shape[dim], axis=dim)
        cells = jnp.concatenate(
            [
                lax.ppermute(tail, axis, [(i, (i + 1) % count) for i in range(ends)]),
                cells,
                lax.ppermute(head, axis, [((i + 1) % count, i) for i in range(ends)]),
            ],
            axis=dim,
        )
    return cells


def make_filters(filter_taps, lat_ext, lon_count):
    lat_reach = filter_taps.shape[2] // 2
    half_width = filter_taps.shape[3] // 2
    lat_dist = jnp.abs(jnp.arange(filter_taps.shape[2], dtype=jnp.int32) - lat_reach)
    lon_dist = jnp.abs(jnp.arange(filter_taps.shape[3], dtype=jnp.int32) - half_width)
    support = (lat_dist[None, :, None] < lat_ext[:, None, None]) & (
        lon_dist[None, None, :] < lon_count[:, None, None]
    )
    support_size = ((2 * lat_ext - 1) * (2 * lon_count - 1)).astype(jnp.float32)
    row_scale = lax.rsqrt(support_size)
    masked = (
        filter_taps.astype(jnp.float32)
        * support[:, None].astype(jnp.float32)
        * row_scale[:, None, None, None]
    )
    return masked.astype(jnp.bfloat16)


def forward_taps(row_taps, lon_width):
    leading = row_taps.shape[:-1]
    return jnp.concatenate(
        [row_taps, jnp.zeros(leading + (lon_width + 1,), row_taps.dtype)], axis=-1
    )


def reverse_taps(row_taps, lon_width):
    leading = row_taps.shape[:-1]
    return jnp.concatenate(
        [
            jnp.zeros(leading + (1,), row_taps.dtype),
            row_taps[..., ::-1],
            jnp.zeros(leading + (lon_width,), row_taps.dtype),
        ],
        axis=-1,
    )


def band_matrix(padded, lon_width):
    leading = padded.shape[:-1]
    repeated = jnp.tile(padded, (1,) * len(leading) + (lon_width,))
    return repeated[..., : lon_width * 3 * lon_width].reshape(leading + (lon_width, 3 * lon_width))


def gather_adjoint(filter_rims, basis_rows, row_count, lon_width, channels, basis_count, lat_taps):
    last = lat_taps - 1
    diagonal = jnp.stack(
        [
            filter_rims[last - offset : last - offset + row_count, :, offset]
            for offset in range(lat_taps)
        ],
        axis=2,
    )
    banded = band_matrix(reverse_taps(diagonal, lon_width), lon_width)
    total_grad = jnp.zeros((row_count, lon_width, channels), jnp.float32)
    for basis_index in range(basis_count):
        grad_window = basis_rows(basis_index)
        patches = jnp.stack(
            [grad_window[last - offset : last - offset + row_count] for offset in range(lat_taps)],
            axis=1,
        )
        total_grad = total_grad + jnp.einsum(
            "oejn,oenc->ojc", banded[:, basis_index], patches, preferred_element_type=jnp.float32
        )
    return total_grad


def per_device(features, cotangent, weight, filter_taps, lat_ext, lon_count):
    row_count, lon_width, channels = features.shape
    basis_count = weight.shape[0]
    lat_taps = filter_taps.shape[2]
    lat_reach = lat_taps // 2
    filters = make_filters(filter_taps, lat_ext, lon_count)
    band_rows = extended(features, (("lat", 0),), lat_reach, False)
    window = extended(band_rows, (("lon", 1),), lon_width, True)
    banded_all = band_matrix(forward_taps(filters, lon_width), lon_width)
    patches = jnp.stack([window[offset : offset + row_count] for offset in range(lat_taps)], axis=1)
    basis_f32 = jnp.einsum(
        "okejm,oemc->ojkc", banded_all, patches, preferred_element_type=jnp.float32
    )
    basis_out = basis_f32.astype(jnp.bfloat16)
    flat_out = basis_out.reshape(row_count * lon_width, basis_count * channels)
    flat_weight = weight.reshape(basis_count * channels, channels)
    output = jnp.dot(flat_out, flat_weight, preferred_element_type=jnp.float32).astype(jnp.bfloat16)
    output = output.reshape(row_count, lon_width, channels)
    flat_cot = cotangent.reshape(row_count * lon_width, channels)
    partial_grad = lax.dot_general(
        flat_out, flat_cot, (((0,), (0,)), ((), ())), preferred_element_type=jnp.float32
    )
    total_cells = row_count * lax.axis_size("lat") * lon_width * lax.axis_size("lon")
    summed_grad = lax.psum(partial_grad, ("lat", "lon"))
    weight_grad = (summed_grad * (1.0 / math.sqrt(total_cells))).reshape(
        basis_count, channels, channels
    )
    filter_rims = extended(filters, (("lat", 0),), lat_reach, False)

    def received_rows(basis_index):
        own_grad = lax.dot_general(
            flat_cot,
            weight[basis_index],
            (((1,), (1,)), ((), ())),
            preferred_element_type=jnp.float32,
        ).astype(jnp.bfloat16)
        own_grad = own_grad.reshape(row_count, lon_width, channels)
        grad_band = extended(own_grad, (("lat", 0),), lat_reach, False)
        return extended(grad_band, (("lon", 1),), lon_width, True)

    field_grad = gather_adjoint(
        filter_rims, received_rows, row_count, lon_width, channels, basis_count, lat_taps
    ).astype(jnp.bfloat16)
    return (output, field_grad, weight_grad)


def solution(mesh):
    in_specs = (
        P("lat", "lon", None),
        P("lat", "lon", None),
        P(),
        P("lat", None, None, None),
        P("lat"),
        P("lat"),
    )
    out_specs = (P("lat", "lon", None), P("lat", "lon", None), P())
    return jax.shard_map(
        per_device, mesh=mesh, in_specs=in_specs, out_specs=out_specs, check_vma=False
    )
```

profile of v0, /device:TPU:1, one launch (start us, length us, event | category | flops | bytes accessed | tf_op | source)
XLA Modules:
  0.0 597.4 jit_solution(2804473898359303226)
XLA Ops:
  7.2 0.8 copy-done
  8.0 1.1 convolution_convert_fusion.4
  9.1 0.6 fusion.43
  9.7 4.6 collective-permute-start.6
  14.3 5.5 collective-permute-start.7
  19.8 0.7 broadcast_compare_fusion
  20.5 0.7 convert_rsqrt_fusion
  21.2 0.7 broadcast_compare_fusion.1
  22.0 0.8 multiply_convert_fusion
  22.8 1.9 collective-permute-start.4
  24.8 3.6 collective-permute-start.5
  28.4 0.2 convolution_convert_fusion.3
  28.6 0.6 fusion.42
  29.3 1.9 collective-permute-start.10
  31.2 0.2 convolution_convert_fusion.2
  31.4 0.2 convolution_convert_fusion.1
  31.6 0.6 fusion.41
  32.2 0.8 copy-done.8
  33.0 0.6 fusion.44
  33.8 0.1 tile.8
  33.9 1.8 tile.9
  35.7 0.2 slice.249
  35.9 0.5 reshape.131
  36.4 2.4 collective-permute-start.11
  38.9 3.2 collective-permute-start.14
  42.1 0.1 rev.3
  42.2 0.1 maximum_maximum_fusion
  42.3 0.1 tile.20
  42.4 1.8 tile.21
  44.2 0.2 slice.253
  44.4 0.5 reshape.135
  44.9 0.2 copy-done.10
  45.1 1.9 collective-permute-start.15
  47.0 3.6 collective-permute-start.18
  50.7 1.9 collective-permute-start.19
  52.7 3.6 collective-permute-start
  56.4 1.0 collective-permute-done
  57.3 1.9 collective-permute-start.1
  59.3 1.9 collective-permute-start.8
  61.2 10.9 %collective-permute-start.9 = (bf16[8,32,256]{2,1,0:T(8,128)(2,1)S(1)}, bf16[8,32,256]{2,1,0:T(8,128)(2,1)S(1)}, u32[]{:S(2)}, u32[]{:S(2)}) collective-permute-start(bf16[8,32,256]{2,1,0:T(8,128)(2,1)S(1)} %pad_maximum_fusion.5), channel_id=1, source_target_pairs={{1,0},{2,1},{3,2},{4,3},{5,4},{6,5},{7,6},{8,7},{9,8},{10,9},{11,1... | collective-permute-start | bytes 393224 | tf_op jit(solution)/shard_map/ppermute | solution.py:18
  72.2 1.9 collective-permute-start.12
  74.1 7.0 %collective-permute-start.13 = (bf16[8,32,256]{2,1,0:T(8,128)(2,1)S(1)}, bf16[8,32,256]{2,1,0:T(8,128)(2,1)S(1)}, u32[]{:S(2)}, u32[]{:S(2)}) collective-permute-start(bf16[8,32,256]{2,1,0:T(8,128)(2,1)S(1)} %pad_maximum_fusion.6), channel_id=1, source_target_pairs={{1,0},{2,1},{3,2},{4,3},{5,4},{6,5},{7,6},{8,7},{9,8},{10,9},{11,1... | collective-permute-start | bytes 393224 | tf_op jit(solution)/shard_map/ppermute | solution.py:18
  81.1 1.9 collective-permute-start.16
  83.1 7.0 %collective-permute-start.17 = (bf16[8,32,256]{2,1,0:T(8,128)(2,1)S(1)}, bf16[8,32,256]{2,1,0:T(8,128)(2,1)S(1)}, u32[]{:S(2)}, u32[]{:S(2)}) collective-permute-start(bf16[8,32,256]{2,1,0:T(8,128)(2,1)S(1)} %pad_maximum_fusion.7), channel_id=1, source_target_pairs={{1,0},{2,1},{3,2},{4,3},{5,4},{6,5},{7,6},{8,7},{9,8},{10,9},{11,1... | collective-permute-start | bytes 393224 | tf_op jit(solution)/shard_map/ppermute | solution.py:18
  90.1 1.9 collective-permute-start.20
  92.1 7.0 %collective-permute-start.21 = (bf16[8,32,256]{2,1,0:T(8,128)(2,1)S(1)}, bf16[8,32,256]{2,1,0:T(8,128)(2,1)S(1)}, u32[]{:S(2)}, u32[]{:S(2)}) collective-permute-start(bf16[8,32,256]{2,1,0:T(8,128)(2,1)S(1)} %pad_maximum_fusion.8), channel_id=1, source_target_pairs={{1,0},{2,1},{3,2},{4,3},{5,4},{6,5},{7,6},{8,7},{9,8},{10,9},{11,1... | collective-permute-start | bytes 393224 | tf_op jit(solution)/shard_map/ppermute | solution.py:18
  99.1 1.9 collective-permute-start.2
  101.2 7.0 %collective-permute-start.3 = (bf16[8,32,256]{2,1,0:T(8,128)(2,1)S(1)}, bf16[8,32,256]{2,1,0:T(8,128)(2,1)S(1)}, u32[]{:S(2)}, u32[]{:S(2)}) collective-permute-start(bf16[8,32,256]{2,1,0:T(8,128)(2,1)S(1)} %constant_dynamic-update-slice_fusion), channel_id=1, source_target_pairs={{1,0},{2,1},{3,2},{4,3},{5,4},{6,5},{7,6},{8,7},{9,8},{10,9},{11,1... | collective-permute-start | bytes 393224 | tf_op jit(solution)/shard_map/ppermute | solution.py:18
  108.4 0.9 copy-done.4
  109.5 0.3 collective-permute-done.2
  109.8 0.6 copy-done.6
  110.4 0.4 collective-permute-done.3
  111.0 0.4 fusion.1
  111.3 0.2 copy.36
  111.6 1.3 fusion.46
  112.9 0.9 convolution_convert_fusion
  113.8 0.3 convolution_bitcast_fusion.4
  114.1 0.3 fusion.4
  114.5 0.6 copy-done.7
  115.1 0.3 copy-done.5
  115.4 0.3 fusion.3
  115.7 1.0 fusion.5
  116.7 471.6 %all-reduce.3.cloned.1.call-done = f32[1024,256]{1,0:T(8,128)} async-done(((f32[1024,256]{1,0:T(8,128)}), f32[1024,256]{1,0:T(8,128)}) %all-reduce.3.cloned.1.call-update) | async-done | bytes 1048592 | tf_op jit(solution)/shard_map/psum | solution.py:114
  588.3 2.3 broadcast_multiply_fusion
  (90 shorter events, 1.1 us)
Async XLA Ops:
  7.2 0.8 copy-start
  7.2 21.2 %copy-start.1 = (bf16[4,256,256]{2,1,0:T(8,128)(2,1)S(1)}, bf16[4,256,256]{2,1,0:T(8,128)(2,1)}, u32[]{:S(2)}) copy-start(bf16[4,256,256]{2,1,0:T(8,128)(2,1)} %param.8) | copy-start | bytes 1572868
  7.2 581.1 %all-reduce.3.cloned.1.call-start = ((), (), s32[]{:S(2)}) async-start(), calls=%async_computation | async-start | bytes 2097152 | tf_op jit(solution)/shard_map/psum | solution.py:114
  9.7 35.1 %collective-permute-start.6 = (bf16[2,32,256]{2,1,0:T(8,128)(2,1)}, bf16[2,32,256]{2,1,0:T(8,128)(2,1)S(1)}, u32[]{:S(2)}, u32[]{:S(2)}) collective-permute-start(bf16[2,32,256]{2,1,0:T(8,128)(2,1)} %bitcast.19), channel_id=1, source_target_pairs={{0,32},{32,64},{64,96},{96,128},{128,160},{160,192},{192,224},{224... | collective-permute-start | bytes 98312 | tf_op jit(solution)/shard_map/ppermute | solution.py:16
  14.3 32.7 %collective-permute-start.7 = (bf16[2,32,256]{2,1,0:T(8,128)(2,1)}, bf16[2,32,256]{2,1,0:T(8,128)(2,1)S(1)}, u32[]{:S(2)}, u32[]{:S(2)}) collective-permute-start(bf16[2,32,256]{2,1,0:T(8,128)(2,1)} %bitcast.21), channel_id=1, source_target_pairs={{32,0},{64,32},{96,64},{128,96},{160,128},{192,160},{224,192},{256... | collective-permute-start | bytes 98312 | tf_op jit(solution)/shard_map/ppermute | solution.py:18
  22.8 13.5 %collective-permute-start.4 = (bf16[2,4,5,64]{3,1,2,0:T(4,128)(2,1)S(1)}, bf16[2,4,5,64]{3,1,2,0:T(4,128)(2,1)S(1)}, u32[]{:S(2)}, u32[]{:S(2)}) collective-permute-start(bf16[2,4,5,64]{3,1,2,0:T(4,128)(2,1)S(1)} %get-tuple-element.14), channel_id=1, source_target_pairs={{32,0},{64,32},{96,64},{128,96},{160,128},{192,160},{224,192},{256... | collective-permute-start | bytes 15368 | tf_op jit(solution)/shard_map/ppermute | solution.py:18
  24.8 14.1 %collective-permute-start.5 = (bf16[2,4,5,64]{3,1,2,0:T(4,128)(2,1)S(1)}, bf16[2,4,5,64]{3,1,2,0:T(4,128)(2,1)S(1)}, u32[]{:S(2)}, u32[]{:S(2)}) collective-permute-start(bf16[2,4,5,64]{3,1,2,0:T(4,128)(2,1)S(1)} %get-tuple-element.13), channel_id=1, source_target_pairs={{0,32},{32,64},{64,96},{96,128},{128,160},{160,192},{192,224},{224... | collective-permute-start | bytes 15368 | tf_op jit(solution)/shard_map/ppermute | solution.py:16
  29.3 21.5 %collective-permute-start.10 = (bf16[2,32,256]{2,1,0:T(8,128)(2,1)}, bf16[2,32,256]{2,1,0:T(8,128)(2,1)S(1)}, u32[]{:S(2)}, u32[]{:S(2)}) collective-permute-start(bf16[2,32,256]{2,1,0:T(8,128)(2,1)} %bitcast.35), channel_id=1, source_target_pairs={{0,32},{32,64},{64,96},{96,128},{128,160},{160,192},{192,224},{224... | collective-permute-start | bytes 98312 | tf_op jit(solution)/shard_map/ppermute | solution.py:16
  32.2 0.8 copy-start.8
  36.4 16.3 %collective-permute-start.11 = (bf16[2,32,256]{2,1,0:T(8,128)(2,1)}, bf16[2,32,256]{2,1,0:T(8,128)(2,1)S(1)}, u32[]{:S(2)}, u32[]{:S(2)}) collective-permute-start(bf16[2,32,256]{2,1,0:T(8,128)(2,1)} %bitcast.37), channel_id=1, source_target_pairs={{32,0},{64,32},{96,64},{128,96},{160,128},{192,160},{224,192},{256... | collective-permute-start | bytes 98312 | tf_op jit(solution)/shard_map/ppermute | solution.py:18
  38.9 20.4 %collective-permute-start.14 = (bf16[2,32,256]{2,1,0:T(8,128)(2,1)}, bf16[2,32,256]{2,1,0:T(8,128)(2,1)S(1)}, u32[]{:S(2)}, u32[]{:S(2)}) collective-permute-start(bf16[2,32,256]{2,1,0:T(8,128)(2,1)} %bitcast.51), channel_id=1, source_target_pairs={{0,32},{32,64},{64,96},{96,128},{128,160},{160,192},{192,224},{224... | collective-permute-start | bytes 98312 | tf_op jit(solution)/shard_map/ppermute | solution.py:16
  44.4 0.8 copy-start.10
  45.1 16.1 %collective-permute-start.15 = (bf16[2,32,256]{2,1,0:T(8,128)(2,1)S(1)}, bf16[2,32,256]{2,1,0:T(8,128)(2,1)S(1)}, u32[]{:S(2)}, u32[]{:S(2)}) collective-permute-start(bf16[2,32,256]{2,1,0:T(8,128)(2,1)S(1)} %bitcast.276), channel_id=1, source_target_pairs={{32,0},{64,32},{96,64},{128,96},{160,128},{192,160},{224,192},{256... | collective-permute-start | bytes 98312 | tf_op jit(solution)/shard_map/ppermute | solution.py:18
  47.0 27.1 %collective-permute-start.18 = (bf16[2,32,256]{2,1,0:T(8,128)(2,1)S(1)}, bf16[2,32,256]{2,1,0:T(8,128)(2,1)S(1)}, u32[]{:S(2)}, u32[]{:S(2)}) collective-permute-start(bf16[2,32,256]{2,1,0:T(8,128)(2,1)S(1)} %bitcast.275), channel_id=1, source_target_pairs={{0,32},{32,64},{64,96},{96,128},{128,160},{160,192},{192,224},{224... | collective-permute-start | bytes 98312 | tf_op jit(solution)/shard_map/ppermute | solution.py:16
  50.7 2.0 copy-start.11
  50.7 30.4 %collective-permute-start.19 = (bf16[2,32,256]{2,1,0:T(8,128)(2,1)S(1)}, bf16[2,32,256]{2,1,0:T(8,128)(2,1)S(1)}, u32[]{:S(2)}, u32[]{:S(2)}) collective-permute-start(bf16[2,32,256]{2,1,0:T(8,128)(2,1)S(1)} %bitcast.274), channel_id=1, source_target_pairs={{32,0},{64,32},{96,64},{128,96},{160,128},{192,160},{224,192},{256... | collective-permute-start | bytes 98312 | tf_op jit(solution)/shard_map/ppermute | solution.py:18
  52.7 4.7 collective-permute-start
  56.3 1.0 copy-start.9
  57.3 14.8 %collective-permute-start.1 = (bf16[2,32,256]{2,1,0:T(8,128)(2,1)S(1)}, bf16[2,32,256]{2,1,0:T(8,128)(2,1)S(1)}, u32[]{:S(2)}, u32[]{:S(2)}) collective-permute-start(bf16[2,32,256]{2,1,0:T(8,128)(2,1)S(1)} %copy-done.9), channel_id=1, source_target_pairs={{32,0},{64,32},{96,64},{128,96},{160,128},{192,160},{224,192},{256... | collective-permute-start | bytes 98312 | tf_op jit(solution)/shard_map/ppermute | solution.py:18
  59.3 23.8 %collective-permute-start.8 = (bf16[8,32,256]{2,1,0:T(8,128)(2,1)S(1)}, bf16[8,32,256]{2,1,0:T(8,128)(2,1)S(1)}, u32[]{:S(2)}, u32[]{:S(2)}) collective-permute-start(bf16[8,32,256]{2,1,0:T(8,128)(2,1)S(1)} %pad_maximum_fusion.5), channel_id=1, source_target_pairs={{0,1},{1,2},{2,3},{3,4},{4,5},{5,6},{6,7},{7,8},{8,9},{9,10},{10,1... | collective-permute-start | bytes 393224 | tf_op jit(solution)/shard_map/ppermute | solution.py:16
  61.2 28.8 %collective-permute-start.9 = (bf16[8,32,256]{2,1,0:T(8,128)(2,1)S(1)}, bf16[8,32,256]{2,1,0:T(8,128)(2,1)S(1)}, u32[]{:S(2)}, u32[]{:S(2)}) collective-permute-start(bf16[8,32,256]{2,1,0:T(8,128)(2,1)S(1)} %pad_maximum_fusion.5), channel_id=1, source_target_pairs={{1,0},{2,1},{3,2},{4,3},{5,4},{6,5},{7,6},{8,7},{9,8},{10,9},{11,1... | collective-permute-start | bytes 393224 | tf_op jit(solution)/shard_map/ppermute | solution.py:18
  72.2 20.0 %collective-permute-start.12 = (bf16[8,32,256]{2,1,0:T(8,128)(2,1)S(1)}, bf16[8,32,256]{2,1,0:T(8,128)(2,1)S(1)}, u32[]{:S(2)}, u32[]{:S(2)}) collective-permute-start(bf16[8,32,256]{2,1,0:T(8,128)(2,1)S(1)} %pad_maximum_fusion.6), channel_id=1, source_target_pairs={{0,1},{1,2},{2,3},{3,4},{4,5},{5,6},{6,7},{7,8},{8,9},{9,10},{10,1... | collective-permute-start | bytes 393224 | tf_op jit(solution)/shard_map/ppermute | solution.py:16
  74.1 25.0 %collective-permute-start.13 = (bf16[8,32,256]{2,1,0:T(8,128)(2,1)S(1)}, bf16[8,32,256]{2,1,0:T(8,128)(2,1)S(1)}, u32[]{:S(2)}, u32[]{:S(2)}) collective-permute-start(bf16[8,32,256]{2,1,0:T(8,128)(2,1)S(1)} %pad_maximum_fusion.6), channel_id=1, source_target_pairs={{1,0},{2,1},{3,2},{4,3},{5,4},{6,5},{7,6},{8,7},{9,8},{10,9},{11,1... | collective-permute-start | bytes 393224 | tf_op jit(solution)/shard_map/ppermute | solution.py:18
  81.1 20.1 %collective-permute-start.16 = (bf16[8,32,256]{2,1,0:T(8,128)(2,1)S(1)}, bf16[8,32,256]{2,1,0:T(8,128)(2,1)S(1)}, u32[]{:S(2)}, u32[]{:S(2)}) collective-permute-start(bf16[8,32,256]{2,1,0:T(8,128)(2,1)S(1)} %pad_maximum_fusion.7), channel_id=1, source_target_pairs={{0,1},{1,2},{2,3},{3,4},{4,5},{5,6},{6,7},{7,8},{8,9},{9,10},{10,1... | collective-permute-start | bytes 393224 | tf_op jit(solution)/shard_map/ppermute | solution.py:16
  83.1 25.2 %collective-permute-start.17 = (bf16[8,32,256]{2,1,0:T(8,128)(2,1)S(1)}, bf16[8,32,256]{2,1,0:T(8,128)(2,1)S(1)}, u32[]{:S(2)}, u32[]{:S(2)}) collective-permute-start(bf16[8,32,256]{2,1,0:T(8,128)(2,1)S(1)} %pad_maximum_fusion.7), channel_id=1, source_target_pairs={{1,0},{2,1},{3,2},{4,3},{5,4},{6,5},{7,6},{8,7},{9,8},{10,9},{11,1... | collective-permute-start | bytes 393224 | tf_op jit(solution)/shard_map/ppermute | solution.py:18
  90.1 18.4 %collective-permute-start.20 = (bf16[8,32,256]{2,1,0:T(8,128)(2,1)S(1)}, bf16[8,32,256]{2,1,0:T(8,128)(2,1)S(1)}, u32[]{:S(2)}, u32[]{:S(2)}) collective-permute-start(bf16[8,32,256]{2,1,0:T(8,128)(2,1)S(1)} %pad_maximum_fusion.8), channel_id=1, source_target_pairs={{0,1},{1,2},{2,3},{3,4},{4,5},{5,6},{6,7},{7,8},{8,9},{9,10},{10,1... | collective-permute-start | bytes 393224 | tf_op jit(solution)/shard_map/ppermute | solution.py:16
  92.1 17.2 %collective-permute-start.21 = (bf16[8,32,256]{2,1,0:T(8,128)(2,1)S(1)}, bf16[8,32,256]{2,1,0:T(8,128)(2,1)S(1)}, u32[]{:S(2)}, u32[]{:S(2)}) collective-permute-start(bf16[8,32,256]{2,1,0:T(8,128)(2,1)S(1)} %pad_maximum_fusion.8), channel_id=1, source_target_pairs={{1,0},{2,1},{3,2},{4,3},{5,4},{6,5},{7,6},{8,7},{9,8},{10,9},{11,1... | collective-permute-start | bytes 393224 | tf_op jit(solution)/shard_map/ppermute | solution.py:18
  99.1 10.6 %collective-permute-start.2 = (bf16[8,32,256]{2,1,0:T(8,128)(2,1)S(1)}, bf16[8,32,256]{2,1,0:T(8,128)(2,1)S(1)}, u32[]{:S(2)}, u32[]{:S(2)}) collective-permute-start(bf16[8,32,256]{2,1,0:T(8,128)(2,1)S(1)} %constant_dynamic-update-slice_fusion), channel_id=1, source_target_pairs={{0,1},{1,2},{2,3},{3,4},{4,5},{5,6},{6,7},{7,8},{8,9},{9,10},{10,1... | collective-permute-start | bytes 393224 | tf_op jit(solution)/shard_map/ppermute | solution.py:16
  101.2 7.0 %copy-start.2 = (bf16[4,5,96,256]{3,2,1,0:T(8,128)(2,1)}, bf16[4,5,96,256]{3,2,1,0:T(8,128)(2,1)S(1)}, u32[]{:S(2)}) copy-start(bf16[4,5,96,256]{3,2,1,0:T(8,128)(2,1)S(1)} %fusion.17) | copy-start | bytes 2949124
  101.2 9.6 %collective-permute-start.3 = (bf16[8,32,256]{2,1,0:T(8,128)(2,1)S(1)}, bf16[8,32,256]{2,1,0:T(8,128)(2,1)S(1)}, u32[]{:S(2)}, u32[]{:S(2)}) collective-permute-start(bf16[8,32,256]{2,1,0:T(8,128)(2,1)S(1)} %constant_dynamic-update-slice_fusion), channel_id=1, source_target_pairs={{1,0},{2,1},{3,2},{4,3},{5,4},{6,5},{7,6},{8,7},{9,8},{10,9},{11,1... | collective-permute-start | bytes 393224 | tf_op jit(solution)/shard_map/ppermute | solution.py:18
  108.4 0.9 copy-start.4
  109.5 0.9 copy-start.6
  112.9 1.2 copy-start.3
  113.8 1.3 copy-start.7
  114.1 1.3 copy-start.5
Sparse Core Ops, SparseCore 0:
  113.0 475.2 all-reduce.2
where the time goes:
time: 598 us; the launch traced here: 597 us
  waiting for transfers between devices  473 us (79%)
  starting transfers between devices  84.5 us (14%)
  between operations  14.9 us (2%)
  local copies, waits for them, and re-layouts  12.9 us (2%)
  matrix products  6.08 us (1%)
    psum x1, waiting for transfers between devices, per_device(): summed_grad = lax.psum(partial_grad, ('lat', 'lon'))  472 us
    ppermute x11, starting transfers between devices, extended(): lax.ppermute(head, axis, [((i + 1) % count, i) for i in range(ends)])  54.3 us
    ppermute x11, starting transfers between devices, extended(): lax.ppermute(tail, axis, [(i, (i + 1) % count) for i in range(ends)])  30.2 us
  transfers between devices with their start and end apart: 23, of which 4 were waited for; matrix products, arithmetic and copies ran while one was open for 2% of the time, Pallas kernels for 0%

commit v1 on v0

--- a/solution.py
+++ b/solution.py
@@ -111,7 +111,12 @@
         flat_out, flat_cot, (((0,), (0,)), ((), ())), preferred_element_type=jnp.float32
     )
     total_cells = row_count * lax.axis_size("lat") * lon_width * lax.axis_size("lon")
-    summed_grad = lax.psum(partial_grad, ("lat", "lon"))
+
+    def zones_compute(target):
+        then = lax.psum(target, axis_name="lat")
+        return lax.psum(then, axis_name="lon")
+
+    summed_grad = zones_compute(partial_grad)
     weight_grad = (summed_grad * (1.0 / math.sqrt(total_cells))).reshape(
         basis_count, channels, channels
     )

time: 598 us -> 566 us (0.946)
  the two profiles are of different devices: /device:TPU:1 before, /device:TPU:2 now
where the time goes in v1:
time: 566 us; the launch traced here: 565 us
  waiting for transfers between devices  440 us (78%)
  starting transfers between devices  87.8 us (16%)
  between operations  14.9 us (3%)
  local copies, waits for them, and re-layouts  10.6 us (2%)
  matrix products  6.08 us (1%)
    psum x1, waiting for transfers between devices, zones_compute(): return lax.psum(then, axis_name='lon')  310 us
    psum x1, waiting for transfers between devices, zones_compute(): then = lax.psum(target, axis_name='lat')  124 us
    ppermute x11, starting transfers between devices, extended(): lax.ppermute(head, axis, [((i + 1) % count, i) for i in range(ends)])  64 us
    ppermute x11, starting transfers between devices, extended(): lax.ppermute(tail, axis, [(i, (i + 1) % count) for i in range(ends)])  23.8 us
  transfers between devices with their start and end apart: 24, of which 5 were waited for; matrix products, arithmetic and copies ran while one was open for 3% of the time, Pallas kernels for 0%

profile of v1, /device:TPU:2, one launch (start us, length us, event | category | flops | bytes accessed | tf_op | source)
XLA Modules:
  0.0 565.5 jit_solution(13620671712382292068)
XLA Ops:
  7.2 0.0 all-reduce.4.cloned.1.call-start
  7.2 0.8 copy-done
  8.0 1.1 convolution_convert_fusion.4
  9.1 1.9 collective-permute-start.6
  11.1 4.5 collective-permute-start.7
  15.6 0.7 broadcast_compare_fusion
  16.4 0.7 convert_rsqrt_fusion
  17.0 0.7 broadcast_compare_fusion.1
  17.8 0.1 and_convert_fusion
  17.8 0.8 multiply_convert_fusion
  18.7 1.9 collective-permute-start.4
  20.6 2.4 collective-permute-start.5
  23.0 0.2 convolution_convert_fusion.3
  23.2 2.2 collective-permute-start.10
  25.4 0.2 convolution_convert_fusion.2
  25.6 0.2 convolution_convert_fusion.1
  25.9 0.8 copy-done.7
  26.7 0.1 pad.35.clone
  26.8 0.1 tile.8
  26.9 1.8 tile.9
  28.7 0.2 slice.249
  28.9 1.4 reshape.131
  30.2 4.2 collective-permute-start.11
  34.6 1.9 collective-permute-start.14
  36.5 0.1 rev.3
  36.6 0.1 maximum_maximum_fusion
  36.7 0.1 tile.20
  36.8 1.8 tile.21
  38.6 0.2 slice.253
  38.8 0.5 reshape.135
  39.4 4.5 collective-permute-start.15
  43.9 1.9 collective-permute-start.18
  45.9 4.5 collective-permute-start.19
  50.4 1.9 collective-permute-start
  52.4 4.2 collective-permute-done
  56.6 1.9 collective-permute-start.1
  58.5 3.8 collective-permute-start.8
  62.4 12.1 %collective-permute-start.9 = (bf16[8,32,256]{2,1,0:T(8,128)(2,1)S(1)}, bf16[8,32,256]{2,1,0:T(8,128)(2,1)S(1)}, u32[]{:S(2)}, u32[]{:S(2)}) collective-permute-start(bf16[8,32,256]{2,1,0:T(8,128)(2,1)S(1)} %pad_maximum_fusion.5), channel_id=1, source_target_pairs={{1,0},{2,1},{3,2},{4,3},{5,4},{6,5},{7,6},{8,7},{9,8},{10,9},{11,1... | collective-permute-start | bytes 393224 | tf_op jit(solution)/shard_map/ppermute | solution.py:18
  74.5 1.9 collective-permute-start.12
  76.5 7.5 %collective-permute-start.13 = (bf16[8,32,256]{2,1,0:T(8,128)(2,1)S(1)}, bf16[8,32,256]{2,1,0:T(8,128)(2,1)S(1)}, u32[]{:S(2)}, u32[]{:S(2)}) collective-permute-start(bf16[8,32,256]{2,1,0:T(8,128)(2,1)S(1)} %pad_maximum_fusion.6), channel_id=1, source_target_pairs={{1,0},{2,1},{3,2},{4,3},{5,4},{6,5},{7,6},{8,7},{9,8},{10,9},{11,1... | collective-permute-start | bytes 393224 | tf_op jit(solution)/shard_map/ppermute | solution.py:18
  84.0 1.9 collective-permute-start.16
  86.0 7.5 %collective-permute-start.17 = (bf16[8,32,256]{2,1,0:T(8,128)(2,1)S(1)}, bf16[8,32,256]{2,1,0:T(8,128)(2,1)S(1)}, u32[]{:S(2)}, u32[]{:S(2)}) collective-permute-start(bf16[8,32,256]{2,1,0:T(8,128)(2,1)S(1)} %pad_maximum_fusion.7), channel_id=1, source_target_pairs={{1,0},{2,1},{3,2},{4,3},{5,4},{6,5},{7,6},{8,7},{9,8},{10,9},{11,1... | collective-permute-start | bytes 393224 | tf_op jit(solution)/shard_map/ppermute | solution.py:18
  93.6 1.9 collective-permute-start.20
  95.7 7.5 %collective-permute-start.21 = (bf16[8,32,256]{2,1,0:T(8,128)(2,1)S(1)}, bf16[8,32,256]{2,1,0:T(8,128)(2,1)S(1)}, u32[]{:S(2)}, u32[]{:S(2)}) collective-permute-start(bf16[8,32,256]{2,1,0:T(8,128)(2,1)S(1)} %pad_maximum_fusion.8), channel_id=1, source_target_pairs={{1,0},{2,1},{3,2},{4,3},{5,4},{6,5},{7,6},{8,7},{9,8},{10,9},{11,1... | collective-permute-start | bytes 393224 | tf_op jit(solution)/shard_map/ppermute | solution.py:18
  103.2 1.9 collective-permute-start.2
  105.3 7.5 %collective-permute-start.3 = (bf16[8,32,256]{2,1,0:T(8,128)(2,1)S(1)}, bf16[8,32,256]{2,1,0:T(8,128)(2,1)S(1)}, u32[]{:S(2)}, u32[]{:S(2)}) collective-permute-start(bf16[8,32,256]{2,1,0:T(8,128)(2,1)S(1)} %constant_dynamic-update-slice_fusion), channel_id=1, source_target_pairs={{1,0},{2,1},{3,2},{4,3},{5,4},{6,5},{7,6},{8,7},{9,8},{10,9},{11,1... | collective-permute-start | bytes 393224 | tf_op jit(solution)/shard_map/ppermute | solution.py:18
  113.0 0.7 collective-permute-done.2
  113.7 0.2 copy-done.4
  113.9 1.4 collective-permute-done.3
  115.5 1.0 copy-done.6
  116.5 0.3 fusion.1
  116.9 0.2 copy.36
  117.1 1.3 fusion.46
  118.4 0.0 all-reduce.6.cloned.1.call-start
  118.5 0.7 fusion.12
  119.3 124.3 %all-reduce.4.cloned.1.call-done = f32[1024,256]{1,0:T(8,128)} async-done(((f32[1024,256]{1,0:T(8,128)}), f32[1024,256]{1,0:T(8,128)}) %all-reduce.4.cloned.1.call-update) | async-done | bytes 1048592 | tf_op jit(solution)/shard_map/psum | solution.py:116
  243.7 0.3 convolution_bitcast_fusion.4
  244.0 0.9 convolution_convert_fusion
  244.8 0.3 fusion.4
  245.2 0.1 copy-done.5
  245.3 0.3 fusion.3
  245.6 1.0 fusion.5
  246.6 309.8 %all-reduce.6.cloned.1.call-done = f32[1024,256]{1,0:T(8,128)} async-done(((f32[1024,256]{1,0:T(8,128)}), f32[1024,256]{1,0:T(8,128)}) %all-reduce.6.cloned.1.call-update) | async-done | bytes 1048592 | tf_op jit(solution)/shard_map/psum | solution.py:117
  556.4 2.3 broadcast_multiply_fusion
  (85 shorter events, 0.9 us)
Async XLA Ops:
  7.2 0.8 copy-start
  7.2 15.8 %copy-start.1 = (bf16[4,256,256]{2,1,0:T(8,128)(2,1)S(1)}, bf16[4,256,256]{2,1,0:T(8,128)(2,1)}, u32[]{:S(2)}) copy-start(bf16[4,256,256]{2,1,0:T(8,128)(2,1)} %param.8) | copy-start | bytes 1572868
  7.2 236.4 %all-reduce.4.cloned.1.call-start = ((), (), s32[]{:S(2)}) async-start(), calls=%async_computation | async-start | bytes 2097152 | tf_op jit(solution)/shard_map/psum | solution.py:116
  9.1 30.2 %collective-permute-start.6 = (bf16[2,32,256]{2,1,0:T(8,128)(2,1)S(1)}, bf16[2,32,256]{2,1,0:T(8,128)(2,1)S(1)}, u32[]{:S(2)}, u32[]{:S(2)}) collective-permute-start(bf16[2,32,256]{2,1,0:T(8,128)(2,1)S(1)} %bitcast.278), channel_id=1, source_target_pairs={{0,32},{32,64},{64,96},{96,128},{128,160},{160,192},{192,224},{224... | collective-permute-start | bytes 98312 | tf_op jit(solution)/shard_map/ppermute | solution.py:16
  11.1 32.8 %collective-permute-start.7 = (bf16[2,32,256]{2,1,0:T(8,128)(2,1)S(1)}, bf16[2,32,256]{2,1,0:T(8,128)(2,1)S(1)}, u32[]{:S(2)}, u32[]{:S(2)}) collective-permute-start(bf16[2,32,256]{2,1,0:T(8,128)(2,1)S(1)} %bitcast.276), channel_id=1, source_target_pairs={{32,0},{64,32},{96,64},{128,96},{160,128},{192,160},{224,192},{256... | collective-permute-start | bytes 98312 | tf_op jit(solution)/shard_map/ppermute | solution.py:18
  18.7 11.6 %collective-permute-start.4 = (bf16[2,4,5,64]{3,1,2,0:T(4,128)(2,1)S(1)}, bf16[2,4,5,64]{3,1,2,0:T(4,128)(2,1)S(1)}, u32[]{:S(2)}, u32[]{:S(2)}) collective-permute-start(bf16[2,4,5,64]{3,1,2,0:T(4,128)(2,1)S(1)} %get-tuple-element.14), channel_id=1, source_target_pairs={{32,0},{64,32},{96,64},{128,96},{160,128},{192,160},{224,192},{256... | collective-permute-start | bytes 15368 | tf_op jit(solution)/shard_map/ppermute | solution.py:18
  20.6 14.0 %collective-permute-start.5 = (bf16[2,4,5,64]{3,1,2,0:T(4,128)(2,1)S(1)}, bf16[2,4,5,64]{3,1,2,0:T(4,128)(2,1)S(1)}, u32[]{:S(2)}, u32[]{:S(2)}) collective-permute-start(bf16[2,4,5,64]{3,1,2,0:T(4,128)(2,1)S(1)} %get-tuple-element.13), channel_id=1, source_target_pairs={{0,32},{32,64},{64,96},{96,128},{128,160},{160,192},{192,224},{224... | collective-permute-start | bytes 15368 | tf_op jit(solution)/shard_map/ppermute | solution.py:16
  23.2 22.6 %collective-permute-start.10 = (bf16[2,32,256]{2,1,0:T(8,128)(2,1)S(1)}, bf16[2,32,256]{2,1,0:T(8,128)(2,1)S(1)}, u32[]{:S(2)}, u32[]{:S(2)}) collective-permute-start(bf16[2,32,256]{2,1,0:T(8,128)(2,1)S(1)} %bitcast.281), channel_id=1, source_target_pairs={{0,32},{32,64},{64,96},{96,128},{128,160},{160,192},{192,224},{224... | collective-permute-start | bytes 98312 | tf_op jit(solution)/shard_map/ppermute | solution.py:16
  25.9 0.8 copy-start.7
  30.2 20.2 %collective-permute-start.11 = (bf16[2,32,256]{2,1,0:T(8,128)(2,1)S(1)}, bf16[2,32,256]{2,1,0:T(8,128)(2,1)S(1)}, u32[]{:S(2)}, u32[]{:S(2)}) collective-permute-start(bf16[2,32,256]{2,1,0:T(8,128)(2,1)S(1)} %bitcast.280), channel_id=1, source_target_pairs={{32,0},{64,32},{96,64},{128,96},{160,128},{192,160},{224,192},{256... | collective-permute-start | bytes 98312 | tf_op jit(solution)/shard_map/ppermute | solution.py:18
  34.6 23.9 %collective-permute-start.14 = (bf16[2,32,256]{2,1,0:T(8,128)(2,1)S(1)}, bf16[2,32,256]{2,1,0:T(8,128)(2,1)S(1)}, u32[]{:S(2)}, u32[]{:S(2)}) collective-permute-start(bf16[2,32,256]{2,1,0:T(8,128)(2,1)S(1)} %bitcast.279), channel_id=1, source_target_pairs={{0,32},{32,64},{64,96},{96,128},{128,160},{160,192},{192,224},{224... | collective-permute-start | bytes 98312 | tf_op jit(solution)/shard_map/ppermute | solution.py:16
  39.4 23.0 %collective-permute-start.15 = (bf16[2,32,256]{2,1,0:T(8,128)(2,1)S(1)}, bf16[2,32,256]{2,1,0:T(8,128)(2,1)S(1)}, u32[]{:S(2)}, u32[]{:S(2)}) collective-permute-start(bf16[2,32,256]{2,1,0:T(8,128)(2,1)S(1)} %bitcast.277), channel_id=1, source_target_pairs={{32,0},{64,32},{96,64},{128,96},{160,128},{192,160},{224,192},{256... | collective-permute-start | bytes 98312 | tf_op jit(solution)/shard_map/ppermute | solution.py:18
  43.9 32.6 %collective-permute-start.18 = (bf16[2,32,256]{2,1,0:T(8,128)(2,1)S(1)}, bf16[2,32,256]{2,1,0:T(8,128)(2,1)S(1)}, u32[]{:S(2)}, u32[]{:S(2)}) collective-permute-start(bf16[2,32,256]{2,1,0:T(8,128)(2,1)S(1)} %bitcast.275), channel_id=1, source_target_pairs={{0,32},{32,64},{64,96},{96,128},{128,160},{160,192},{192,224},{224... | collective-permute-start | bytes 98312 | tf_op jit(solution)/shard_map/ppermute | solution.py:16
  45.9 38.2 %collective-permute-start.19 = (bf16[2,32,256]{2,1,0:T(8,128)(2,1)S(1)}, bf16[2,32,256]{2,1,0:T(8,128)(2,1)S(1)}, u32[]{:S(2)}, u32[]{:S(2)}) collective-permute-start(bf16[2,32,256]{2,1,0:T(8,128)(2,1)S(1)} %bitcast.274), channel_id=1, source_target_pairs={{32,0},{64,32},{96,64},{128,96},{160,128},{192,160},{224,192},{256... | collective-permute-start | bytes 98312 | tf_op jit(solution)/shard_map/ppermute | solution.py:18
  50.4 6.1 %collective-permute-start = (bf16[2,32,256]{2,1,0:T(8,128)(2,1)S(1)}, bf16[2,32,256]{2,1,0:T(8,128)(2,1)S(1)}, u32[]{:S(2)}, u32[]{:S(2)}) collective-permute-start(bf16[2,32,256]{2,1,0:T(8,128)(2,1)S(1)} %get-tuple-element.12), channel_id=1, source_target_pairs={{0,32},{32,64},{64,96},{96,128},{128,160},{160,192},{192,224},{224... | collective-permute-start | bytes 98312 | tf_op jit(solution)/shard_map/ppermute | solution.py:16
  56.6 18.0 %collective-permute-start.1 = (bf16[2,32,256]{2,1,0:T(8,128)(2,1)S(1)}, bf16[2,32,256]{2,1,0:T(8,128)(2,1)S(1)}, u32[]{:S(2)}, u32[]{:S(2)}) collective-permute-start(bf16[2,32,256]{2,1,0:T(8,128)(2,1)S(1)} %get-tuple-element.11), channel_id=1, source_target_pairs={{32,0},{64,32},{96,64},{128,96},{160,128},{192,160},{224,192},{256... | collective-permute-start | bytes 98312 | tf_op jit(solution)/shard_map/ppermute | solution.py:18
  58.5 27.5 %collective-permute-start.8 = (bf16[8,32,256]{2,1,0:T(8,128)(2,1)S(1)}, bf16[8,32,256]{2,1,0:T(8,128)(2,1)S(1)}, u32[]{:S(2)}, u32[]{:S(2)}) collective-permute-start(bf16[8,32,256]{2,1,0:T(8,128)(2,1)S(1)} %pad_maximum_fusion.5), channel_id=1, source_target_pairs={{0,1},{1,2},{2,3},{3,4},{4,5},{5,6},{6,7},{7,8},{8,9},{9,10},{10,1... | collective-permute-start | bytes 393224 | tf_op jit(solution)/shard_map/ppermute | solution.py:16
  62.4 31.2 %collective-permute-start.9 = (bf16[8,32,256]{2,1,0:T(8,128)(2,1)S(1)}, bf16[8,32,256]{2,1,0:T(8,128)(2,1)S(1)}, u32[]{:S(2)}, u32[]{:S(2)}) collective-permute-start(bf16[8,32,256]{2,1,0:T(8,128)(2,1)S(1)} %pad_maximum_fusion.5), channel_id=1, source_target_pairs={{1,0},{2,1},{3,2},{4,3},{5,4},{6,5},{7,6},{8,7},{9,8},{10,9},{11,1... | collective-permute-start | bytes 393224 | tf_op jit(solution)/shard_map/ppermute | solution.py:18
  74.5 21.1 %collective-permute-start.12 = (bf16[8,32,256]{2,1,0:T(8,128)(2,1)S(1)}, bf16[8,32,256]{2,1,0:T(8,128)(2,1)S(1)}, u32[]{:S(2)}, u32[]{:S(2)}) collective-permute-start(bf16[8,32,256]{2,1,0:T(8,128)(2,1)S(1)} %pad_maximum_fusion.6), channel_id=1, source_target_pairs={{0,1},{1,2},{2,3},{3,4},{4,5},{5,6},{6,7},{7,8},{8,9},{9,10},{10,1... | collective-permute-start | bytes 393224 | tf_op jit(solution)/shard_map/ppermute | solution.py:16
  76.5 26.7 %collective-permute-start.13 = (bf16[8,32,256]{2,1,0:T(8,128)(2,1)S(1)}, bf16[8,32,256]{2,1,0:T(8,128)(2,1)S(1)}, u32[]{:S(2)}, u32[]{:S(2)}) collective-permute-start(bf16[8,32,256]{2,1,0:T(8,128)(2,1)S(1)} %pad_maximum_fusion.6), channel_id=1, source_target_pairs={{1,0},{2,1},{3,2},{4,3},{5,4},{6,5},{7,6},{8,7},{9,8},{10,9},{11,1... | collective-permute-start | bytes 393224 | tf_op jit(solution)/shard_map/ppermute | solution.py:18
  84.0 21.3 %collective-permute-start.16 = (bf16[8,32,256]{2,1,0:T(8,128)(2,1)S(1)}, bf16[8,32,256]{2,1,0:T(8,128)(2,1)S(1)}, u32[]{:S(2)}, u32[]{:S(2)}) collective-permute-start(bf16[8,32,256]{2,1,0:T(8,128)(2,1)S(1)} %pad_maximum_fusion.7), channel_id=1, source_target_pairs={{0,1},{1,2},{2,3},{3,4},{4,5},{5,6},{6,7},{7,8},{8,9},{9,10},{10,1... | collective-permute-start | bytes 393224 | tf_op jit(solution)/shard_map/ppermute | solution.py:16
  86.0 26.9 %collective-permute-start.17 = (bf16[8,32,256]{2,1,0:T(8,128)(2,1)S(1)}, bf16[8,32,256]{2,1,0:T(8,128)(2,1)S(1)}, u32[]{:S(2)}, u32[]{:S(2)}) collective-permute-start(bf16[8,32,256]{2,1,0:T(8,128)(2,1)S(1)} %pad_maximum_fusion.7), channel_id=1, source_target_pairs={{1,0},{2,1},{3,2},{4,3},{5,4},{6,5},{7,6},{8,7},{9,8},{10,9},{11,1... | collective-permute-start | bytes 393224 | tf_op jit(solution)/shard_map/ppermute | solution.py:18
  93.6 25.6 %collective-permute-start.20 = (bf16[8,32,256]{2,1,0:T(8,128)(2,1)S(1)}, bf16[8,32,256]{2,1,0:T(8,128)(2,1)S(1)}, u32[]{:S(2)}, u32[]{:S(2)}) collective-permute-start(bf16[8,32,256]{2,1,0:T(8,128)(2,1)S(1)} %pad_maximum_fusion.8), channel_id=1, source_target_pairs={{0,1},{1,2},{2,3},{3,4},{4,5},{5,6},{6,7},{7,8},{8,9},{9,10},{10,1... | collective-permute-start | bytes 393224 | tf_op jit(solution)/shard_map/ppermute | solution.py:16
  95.7 23.5 %collective-permute-start.21 = (bf16[8,32,256]{2,1,0:T(8,128)(2,1)S(1)}, bf16[8,32,256]{2,1,0:T(8,128)(2,1)S(1)}, u32[]{:S(2)}, u32[]{:S(2)}) collective-permute-start(bf16[8,32,256]{2,1,0:T(8,128)(2,1)S(1)} %pad_maximum_fusion.8), channel_id=1, source_target_pairs={{1,0},{2,1},{3,2},{4,3},{5,4},{6,5},{7,6},{8,7},{9,8},{10,9},{11,1... | collective-permute-start | bytes 393224 | tf_op jit(solution)/shard_map/ppermute | solution.py:18
  103.2 10.5 %collective-permute-start.2 = (bf16[8,32,256]{2,1,0:T(8,128)(2,1)S(1)}, bf16[8,32,256]{2,1,0:T(8,128)(2,1)S(1)}, u32[]{:S(2)}, u32[]{:S(2)}) collective-permute-start(bf16[8,32,256]{2,1,0:T(8,128)(2,1)S(1)} %constant_dynamic-update-slice_fusion), channel_id=1, source_target_pairs={{0,1},{1,2},{2,3},{3,4},{4,5},{5,6},{6,7},{7,8},{8,9},{9,10},{10,1... | collective-permute-start | bytes 393224 | tf_op jit(solution)/shard_map/ppermute | solution.py:16
  105.3 7.6 %copy-start.2 = (bf16[4,5,96,256]{3,2,1,0:T(8,128)(2,1)}, bf16[4,5,96,256]{3,2,1,0:T(8,128)(2,1)S(1)}, u32[]{:S(2)}) copy-start(bf16[4,5,96,256]{3,2,1,0:T(8,128)(2,1)S(1)} %fusion.17) | copy-start | bytes 2949124
  105.3 10.0 %collective-permute-start.3 = (bf16[8,32,256]{2,1,0:T(8,128)(2,1)S(1)}, bf16[8,32,256]{2,1,0:T(8,128)(2,1)S(1)}, u32[]{:S(2)}, u32[]{:S(2)}) collective-permute-start(bf16[8,32,256]{2,1,0:T(8,128)(2,1)S(1)} %constant_dynamic-update-slice_fusion), channel_id=1, source_target_pairs={{1,0},{2,1},{3,2},{4,3},{5,4},{6,5},{7,6},{8,7},{9,8},{10,9},{11,1... | collective-permute-start | bytes 393224 | tf_op jit(solution)/shard_map/ppermute | solution.py:18
  113.0 0.9 copy-start.4
  115.4 1.1 copy-start.6
  118.4 437.9 %all-reduce.6.cloned.1.call-start = ((), (), s32[]{:S(2)}) async-start(), calls=%async_computation.1 | async-start | bytes 2097152 | tf_op jit(solution)/shard_map/psum | solution.py:117
  243.6 1.2 copy-start.3
  244.0 1.3 copy-start.5
Sparse Core Ops, SparseCore 0:
  118.6 125.0 all-reduce.3
  246.5 309.8 all-reduce.5
